TPU v7x, 512 devices: a whole 4x4x16 slice. The times are simulated.
512 devices in a mesh: region: 128 (over z, x, core), pair: 4 (over y).
Axes of the slice: x: 4, y: 4, z: 16, core: 2. Of those that a mesh axis runs over, the one named last changes fastest.
Arguments:
- phi: bfloat16 [1024, 128, 32, 128], P('region', None, 'pair'), may hold values from -0.09375 to 0.09375
- potential: float32 [128, 32, 128], P('region', 'pair'), may hold values from -2 to 2
- pair_list: int32 [32, 2], replicated, may hold values from 0 to 7, as said below
- support: int32 [8, 128], replicated, may hold values 0 or 1
Outputs:
- intersection: float32 [32, 16384], P('pair', 'region')
- hamiltonian: float32 [32, 16384], P('pair', 'region')
- hphi: bfloat16 [1024, 128, 32, 128], P('region', None, 'pair')
Inputs may be any that keep to these rules, and one draw needn't show every extreme that they name: `pair_list`: each row is an ordered pair of block numbers; no pair appears twice.
All inputs are finite; a program needn't handle non-finite values.
Results may differ from a plain program's by a relative error of at most 0.0029.
Values may be sent and summed in bfloat16 or wider, within the bound.
No kernel may reach another device: no remote copies, remote signals or barrier semaphores. Data moves between devices by JAX's collectives and lax.ppermute only.
A program may use at most 64 MiB of HBM per device.

v0:
```python
import jax
import jax.numpy as jnp
from jax import lax
from jax.sharding import PartitionSpec as P

W = 128


def padded_2(block, sides, width):
    for axis, dim in sides:
        count = lax.axis_size(axis)
        forward = [(i, i + 1) for i in range(count - 1)]
        forward.append((count - 1, 0))
        backward = [(target, source) for source, target in forward]
        low = lax.ppermute(
            lax.slice_in_dim(block, block.shape[dim] - width, None, axis=dim), axis, forward
        )
        high = lax.ppermute(lax.slice_in_dim(block, 0, width, axis=dim), axis, backward)
        block = jnp.concatenate([low, block, high], axis=dim)
    return block


def apply_region(padded, potential, keep_value):
    values = padded.astype(jnp.float32)
    center = values[:, 1:-1, 1:-1]
    laplace_sum = values[:, 2:, 1:-1] + values[:, :-2, 1:-1] - 6.0 * center
    laplace_sum = laplace_sum + values[:, 1:-1, 2:] + values[:, 1:-1, :-2]
    z_padded = jnp.pad(center, ((0, 0), (0, 0), (0, 0), (1, 1)))
    laplace_sum = laplace_sum + z_padded[..., 2:] + z_padded[..., :-2]
    applied = (-0.5 * laplace_sum + potential[None] * center) * keep_value
    return applied.astype(jnp.bfloat16)


def local(phi, potential, pair_list, support):
    region_id = lax.axis_index("region")
    block_count = support.shape[0]
    all_funcs = block_count * W
    row_count = phi.shape[2]
    depth = phi.shape[3]
    plane_count = potential.shape[0]
    block_flags = lax.dynamic_slice_in_dim(support, region_id, 1, 1)[:, 0]
    func_live = jnp.repeat(block_flags > 0, W)
    region_data = lax.all_to_all(phi, "region", split_axis=1, concat_axis=0, tiled=True)
    confined = jnp.where(func_live[:, None, None, None], region_data, jnp.zeros_like(region_data))
    padded = padded_2(confined, (("region", 1), ("pair", 2)), 1)
    keep_values = block_flags.astype(jnp.float32)
    stacked = padded.reshape(block_count, W, plane_count + 2, row_count + 2, depth)
    applied_region = lax.map(
        lambda members: apply_region(members[0], potential, members[1]), (stacked, keep_values)
    )
    applied_region = applied_region.reshape(all_funcs, plane_count, row_count, depth)
    cell_count = plane_count * row_count * depth
    flat_data = confined.reshape(all_funcs, cell_count)
    flat_applied = applied_region.reshape(all_funcs, cell_count)
    contract_dims = (((1,), (1,)), ((), ()))

    def pair_terms(pair_row):
        left_rows = lax.dynamic_slice_in_dim(flat_data, pair_row[0] * W, W, 0)
        right_rows = lax.dynamic_slice_in_dim(flat_data, pair_row[1] * W, W, 0)
        ham_rows = lax.dynamic_slice_in_dim(flat_applied, pair_row[1] * W, W, 0)
        return (
            lax.dot_general(
                left_rows, right_rows, contract_dims, preferred_element_type=jnp.float32
            ),
            lax.dot_general(left_rows, ham_rows, contract_dims, preferred_element_type=jnp.float32),
        )

    intersection_part, hamil_part = lax.map(pair_terms, pair_list)
    pair_count = pair_list.shape[0]
    intersection_part = intersection_part.reshape(pair_count, W * W)
    hamil_part = hamil_part.reshape(pair_count, W * W)
    intersection_cols, hamil_cols = (
        lax.psum_scatter(intersection_part, "region", scatter_dimension=1, tiled=True),
        lax.psum_scatter(hamil_part, "region", scatter_dimension=1, tiled=True),
    )
    intersection, hamiltonian = (
        lax.psum_scatter(intersection_cols, "pair", scatter_dimension=0, tiled=True),
        lax.psum_scatter(hamil_cols, "pair", scatter_dimension=0, tiled=True),
    )
    hphi_out = lax.all_to_all(applied_region, "region", split_axis=0, concat_axis=1, tiled=True)
    return (intersection, hamiltonian, hphi_out)


def solution(mesh):
    in_specs = (P("region", None, "pair", None), P("region", "pair", None), P(), P())
    out_specs = (P("pair", "region"), P("pair", "region"), P("region", None, "pair", None))
    return jax.shard_map(local, mesh=mesh, in_specs=in_specs, out_specs=out_specs, check_vma=False)
```

profile of v0, /device:TPU:2, one launch (start us, length us, event | category | flops | bytes accessed | tf_op | source)
XLA Modules:
  0.0 986.6 jit_solution(11047298964091114942)
XLA Ops:
  7.2 3.5 copy.12
  10.7 19.6 %all-to-all-start = ((bf16[8,128,8,128]{3,2,0,1:T(8,128)(2,1)}), bf16[8,128,8,128]{3,2,0,1:T(8,128)(2,1)S(1)}, u32[]{:S(2)}, u32[]{:S(2)}) async-start(bf16[8,128,8,128]{3,2,0,1:T(8,128)(2,1)} %copy.12), calls=%async_computation | async-start | bytes 4194304 | tf_op jit(solution)/shard_map/all_to_all | solution.py:43
  30.5 96.1 %all-to-all-done = bf16[8,128,8,128]{3,2,0,1:T(8,128)(2,1)S(1)} async-done(((bf16[8,128,8,128]{3,2,0,1:T(8,128)(2,1)}), bf16[8,128,8,128]{3,2,0,1:T(8,128)(2,1)S(1)}, u32[]{:S(2)}, u32[]{:S(2)}) %all-to-all-start) | async-done | bytes 2097184 | tf_op jit(solution)/shard_map/all_to_all | solution.py:43
  126.6 3.7 bitcast_select_fusion.1
  130.3 2.7 collective-permute-start
  133.0 2.9 collective-permute-start.1
  135.9 21.8 %collective-permute-done = bf16[1024,1,8,128]{3,2,0,1:T(8,128)(2,1)S(1)} collective-permute-done((bf16[1024,1,8,128]{3,2,0,1:T(8,128)(2,1)S(1)}, bf16[1024,1,8,128]{3,2,0,1:T(8,128)(2,1)S(1)}, u32[]{:S(2)}, u32[]{:S(2)}) %collective-permute-start) | collective-permute-done | bytes 2097184 | tf_op jit(solution)/shard_map/ppermute | solution.py:15
  159.4 2.6 pad_maximum_fusion.3
  162.2 3.5 collective-permute-start.2
  166.7 3.6 collective-permute-start.3
  172.2 13.0 %collective-permute-done.2 = bf16[1024,3,1,128]{3,0,2,1:T(8,128)(2,1)} collective-permute-done((bf16[1024,3,1,128]{3,0,2,1:T(8,128)(2,1)S(1)}, bf16[1024,3,1,128]{3,0,2,1:T(8,128)(2,1)}, u32[]{:S(2)}, u32[]{:S(2)}) %collective-permute-start.2) | collective-permute-done | bytes 786464 | tf_op jit(solution)/shard_map/ppermute | solution.py:15
  185.2 2.3 copy.15
  189.1 2.3 copy.16
  191.5 10.7 %pad_maximum_fusion = bf16[1024,3,10,128]{3,2,0,1:T(8,128)(2,1)} fusion(bf16[1024,3,1,128]{3,2,0,1:T(2,128)(2,1)S(1)} %copy.16, bf16[1024,1,8,128]{3,2,0,1:T(8,128)(2,1)S(1)} %copy-done.7, bf16[1024,1,8,128]{3,2,0,1:T(8,128)(2,1)S(1)} %copy-done.1, bf16[1024,1,8,128]{3,2,0,1:T(8,128)(2,1)S(1)} %copy-done.5, bf16[1024,3,1,128]{3,2,0,1:T(2,128)(2,1)S(1)} %copy.15), kind=kLoop, calls=%fused_computation.25 | loop fusion | flops 39321600 | bytes 15728640 | tf_op jit(solution)/shard_map/concatenate | solution.py:19
  202.2 28.2 %while.24 = (s32[]{:T(128)}, bf16[8,128,1,8,128]{4,3,2,1,0:T(8,128)(2,1)S(1)}, bf16[8,128,3,10,128]{4,3,1,0,2:T(8,128)(2,1)}, f32[1,8,128]{2,1,0:T(8,128)S(1)}, f32[8]{0:T(128)S(1)}, /*index=5*/s32[]{:T(128)}) while((s32[]{:T(128)}, bf16[8,128,1,8,128]{4,3,2,1,0:T(8,128)(2,1)S(1)}, bf16[8,128,3,10,128]{4,3,1,0,2:T(8,128)(2,1)}, ...), condition=%wide.region_1.2_spmd, body=%wide.region_0.1_spmd.sunk | while | flops 2064386 | bytes 6885469 | solution.py:48
  230.4 2.0 copy.33
  232.3 10.9 %all-to-all-start.1 = ((bf16[1024,1,8,128]{3,2,1,0:T(8,128)(2,1)}), bf16[1024,1,8,128]{3,2,1,0:T(8,128)(2,1)S(1)}, u32[]{:S(2)}, u32[]{:S(2)}) async-start(bf16[1024,1,8,128]{3,2,1,0:T(8,128)(2,1)} %bitcast.76), calls=%async_computation.3 | async-start | bytes 4194304 | tf_op jit(solution)/shard_map/all_to_all | solution.py:80
  243.3 186.2 %while.25 = (s32[]{:T(128)}, f32[32,128,128]{2,1,0:T(8,128)}, f32[32,128,128]{2,1,0:T(8,128)}, s32[32,2]{0,1:T(2,128)S(1)}, bf16[1024,1024]{1,0:T(8,128)(2,1)}, ...) while((s32[]{:T(128)}, f32[32,128,128]{2,1,0:T(8,128)}, ...), condition=%wide.region_3.4_spmd, body=%wide.region_2.3_spmd.sunk | while | flops 67108872 | bytes 1180917 | solution.py:68
  251.2 1.9 fusion.29
  253.1 1.9 fusion.28
  257.0 1.9 fusion.29
  258.9 1.9 fusion.28
  262.8 1.9 fusion.29
  264.7 1.9 fusion.28
  268.6 1.9 fusion.29
  274.5 1.9 fusion.29
  280.3 1.9 fusion.29
  286.1 1.9 fusion.29
  291.9 1.9 fusion.29
  297.7 1.9 fusion.29
  299.6 1.9 fusion.28
  303.5 1.9 fusion.29
  305.4 1.9 fusion.28
  309.4 1.9 fusion.29
  315.2 1.9 fusion.29
  317.1 1.9 fusion.28
  326.9 1.9 fusion.29
  328.8 1.9 fusion.28
  338.5 1.9 fusion.29
  344.3 1.9 fusion.29
  346.2 1.9 fusion.28
  350.1 1.9 fusion.29
  352.0 1.9 fusion.28
  367.5 1.9 fusion.29
  369.4 1.9 fusion.28
  373.4 1.9 fusion.29
  379.2 1.9 fusion.29
  385.0 1.9 fusion.29
  386.9 1.9 fusion.28
  390.8 1.9 fusion.29
  392.7 1.9 fusion.28
  396.6 1.9 fusion.29
  402.5 1.9 fusion.29
  408.3 1.9 fusion.29
  414.1 1.9 fusion.29
  416.0 1.9 fusion.28
  419.9 1.9 fusion.29
  421.8 1.9 fusion.28
  425.7 1.9 fusion.29
  429.5 4.1 copy.32
  433.7 4.1 copy.31
  439.8 255.7 %reduce-scatter.3.cloned.1.call-done = f32[32,128]{1,0:T(8,128)} async-done(((f32[32,16384]{1,0:T(8,128)}), f32[32,128]{1,0:T(8,128)}) %reduce-scatter.3.cloned.1.call-update) | async-done | bytes 16400 | tf_op jit(solution)/shard_map/reduce_scatter | solution.py:73
  695.5 264.2 %reduce-scatter.5.cloned.1.call-done = f32[32,128]{1,0:T(8,128)} async-done(((f32[32,16384]{1,0:T(8,128)}), f32[32,128]{1,0:T(8,128)}) %reduce-scatter.5.cloned.1.call-update) | async-done | bytes 16400 | tf_op jit(solution)/shard_map/reduce_scatter | solution.py:74
  959.7 17.7 %all-reduce.3 = (f32[32,128]{1,0:T(8,128)S(1)}, f32[32,128]{1,0:T(8,128)S(1)}) all-reduce(f32[32,128]{1,0:T(8,128)} %reduce-scatter.3.cloned.1.call-done, f32[32,128]{1,0:T(8,128)} %reduce-scatter.5.cloned.1.call-done), channel_id=3, replica_groups=mesh['region'=128,'pair'=4] {'pair'}, use_global_device_ids=true, to_apply=%region_5.6.clone | all-reduce | flops 8192 | bytes 65536
  (160 shorter events, 103.3 us)
Async XLA Ops:
  10.7 19.6 %copy-start.10 = (s32[8,128]{1,0:T(8,128)S(1)}, s32[8,128]{1,0:T(8,128)}, u32[]{:S(2)}) copy-start(s32[8,128]{1,0:T(8,128)} %param.11) | copy-start | bytes 12292
  10.7 115.9 %all-to-all-start = ((bf16[8,128,8,128]{3,2,0,1:T(8,128)(2,1)}), bf16[8,128,8,128]{3,2,0,1:T(8,128)(2,1)S(1)}, u32[]{:S(2)}, u32[]{:S(2)}) async-start(bf16[8,128,8,128]{3,2,0,1:T(8,128)(2,1)} %copy.12), calls=%async_computation | async-start | bytes 4194304 | tf_op jit(solution)/shard_map/all_to_all | solution.py:43
  130.3 31.8 %copy-start = (bf16[1024,1,8,128]{3,2,0,1:T(8,128)(2,1)}, bf16[1024,1,8,128]{3,2,0,1:T(8,128)(2,1)S(1)}, u32[]{:S(2)}) copy-start(bf16[1024,1,8,128]{3,2,0,1:T(8,128)(2,1)S(1)} %bitcast_select_fusion.1) | copy-start | bytes 6291460
  130.3 27.4 %collective-permute-start = (bf16[1024,1,8,128]{3,2,0,1:T(8,128)(2,1)S(1)}, bf16[1024,1,8,128]{3,2,0,1:T(8,128)(2,1)S(1)}, u32[]{:S(2)}, u32[]{:S(2)}) collective-permute-start(bf16[1024,1,8,128]{3,2,0,1:T(8,128)(2,1)S(1)} %bitcast_select_fusion.1), channel_id=1, source_target_pairs={{0,4},{4,8},{8,12},{12,16},{16,20},{20,24},{24,28},{28,32},{32,36}... | collective-permute-start | bytes 6291464 | tf_op jit(solution)/shard_map/ppermute | solution.py:15
  133.0 26.4 %collective-permute-start.1 = (bf16[1024,1,8,128]{3,2,0,1:T(8,128)(2,1)S(1)}, bf16[1024,1,8,128]{3,2,0,1:T(8,128)(2,1)S(1)}, u32[]{:S(2)}, u32[]{:S(2)}) collective-permute-start(bf16[1024,1,8,128]{3,2,0,1:T(8,128)(2,1)S(1)} %bitcast_select_fusion.1), channel_id=1, source_target_pairs={{4,0},{8,4},{12,8},{16,12},{20,16},{24,20},{28,24},{32,28},{36,32}... | collective-permute-start | bytes 6291464 | tf_op jit(solution)/shard_map/ppermute | solution.py:18
  157.7 4.4 copy-start.4
  159.4 2.7 copy-start.6
  162.2 23.0 %collective-permute-start.2 = (bf16[1024,3,1,128]{3,0,2,1:T(8,128)(2,1)S(1)}, bf16[1024,3,1,128]{3,0,2,1:T(8,128)(2,1)}, u32[]{:S(2)}, u32[]{:S(2)}) collective-permute-start(bf16[1024,3,1,128]{3,0,2,1:T(8,128)(2,1)S(1)} %copy.13), channel_id=1, source_target_pairs={{0,1},{1,2},{2,3},{3,0},{4,5},{5,6},{6,7},{7,4},{8,9},{9,10},{10,1... | collective-permute-start | bytes 2359304 | tf_op jit(solution)/shard_map/ppermute | solution.py:15
  166.7 22.4 %collective-permute-start.3 = (bf16[1024,3,1,128]{3,0,2,1:T(8,128)(2,1)}, bf16[1024,3,1,128]{3,0,2,1:T(8,128)(2,1)}, u32[]{:S(2)}, u32[]{:S(2)}) collective-permute-start(bf16[1024,3,1,128]{3,0,2,1:T(8,128)(2,1)} %copy.14), channel_id=1, source_target_pairs={{1,0},{2,1},{3,2},{0,3},{5,4},{6,5},{7,6},{4,7},{9,8},{10,9},{11,1... | collective-permute-start | bytes 2359304 | tf_op jit(solution)/shard_map/ppermute | solution.py:18
  170.5 20.9 %copy-start.7 = (bf16[1024,1,8,128]{3,2,0,1:T(8,128)(2,1)S(1)}, bf16[1024,1,8,128]{3,2,0,1:T(8,128)(2,1)}, u32[]{:S(2)}) copy-start(bf16[1024,1,8,128]{3,2,0,1:T(8,128)(2,1)} %copy-done.6) | copy-start | bytes 6291460
  172.2 19.2 %copy-start.1 = (bf16[1024,1,8,128]{3,2,0,1:T(8,128)(2,1)S(1)}, bf16[1024,1,8,128]{3,2,0,1:T(8,128)(2,1)}, u32[]{:S(2)}) copy-start(bf16[1024,1,8,128]{3,2,0,1:T(8,128)(2,1)} %copy-done) | copy-start | bytes 6291460
  172.2 19.2 %copy-start.5 = (bf16[1024,1,8,128]{3,2,0,1:T(8,128)(2,1)S(1)}, bf16[1024,1,8,128]{3,2,0,1:T(8,128)(2,1)}, u32[]{:S(2)}) copy-start(bf16[1024,1,8,128]{3,2,0,1:T(8,128)(2,1)} %copy-done.4) | copy-start | bytes 6291460
  191.4 10.7 %copy-start.2 = (bf16[8,128,1,8,128]{4,3,2,1,0:T(8,128)(2,1)S(1)}, bf16[8,128,1,8,128]{4,3,2,1,0:T(8,128)(2,1)}, u32[]{:S(2)}) copy-start(bf16[8,128,1,8,128]{4,3,2,1,0:T(8,128)(2,1)} %custom-call) | copy-start | bytes 6291460
  191.4 10.7 %copy-start.8 = (f32[1,8,128]{2,1,0:T(8,128)S(1)}, f32[1,8,128]{2,1,0:T(8,128)}, u32[]{:S(2)}) copy-start(f32[1,8,128]{2,1,0:T(8,128)} %param.9) | copy-start | bytes 12292
  230.4 2.0 copy-start.3
  232.3 11.0 %copy-start.9 = (s32[32,2]{0,1:T(2,128)S(1)}, s32[32,2]{0,1:T(2,128)}, u32[]{:S(2)}) copy-start(s32[32,2]{0,1:T(2,128)} %param.10) | copy-start | bytes 772
  232.3 745.7 %all-to-all-start.1 = ((bf16[1024,1,8,128]{3,2,1,0:T(8,128)(2,1)}), bf16[1024,1,8,128]{3,2,1,0:T(8,128)(2,1)S(1)}, u32[]{:S(2)}, u32[]{:S(2)}) async-start(bf16[1024,1,8,128]{3,2,1,0:T(8,128)(2,1)} %bitcast.76), calls=%async_computation.3 | async-start | bytes 4194304 | tf_op jit(solution)/shard_map/all_to_all | solution.py:80
  243.3 452.2 %reduce-scatter.3.cloned.1.call-start = ((), (), s32[]{:S(2)}) async-start(), calls=%async_computation.4 | async-start | bytes 2113536 | tf_op jit(solution)/shard_map/reduce_scatter | solution.py:73
  433.7 526.0 %reduce-scatter.5.cloned.1.call-start = ((), (), s32[]{:S(2)}) async-start(), calls=%async_computation.5 | async-start | bytes 2113536 | tf_op jit(solution)/shard_map/reduce_scatter | solution.py:74
Sparse Core Ops, SparseCore 0:
  433.8 261.6 reduce-scatter.2
  700.7 259.0 reduce-scatter.4
where the time goes:
time: 989 us; the launch traced here: 987 us
  waiting for transfers between devices  654 us (66%)
  matrix products  121 us (12%)
  local copies, waits for them, and re-layouts  50.4 us (5%)
  loops' own time  43.5 us (4%)
  starting transfers between devices  43.2 us (4%)
  other arithmetic  41.4 us (4%)
  blocking collectives  17.7 us (2%)
  between operations  14.9 us (2%)
    reduce_scatter x1, waiting for transfers between devices, local(): lax.psum_scatter(hamil_part, 'region', scatter_dimension=1, tiled=True)  264 us
    reduce_scatter x1, waiting for transfers between devices, local(): lax.psum_scatter(intersection_part, 'region', scatter_dimension=1, tiled=...  256 us
    all_to_all x1, waiting for transfers between devices, local(): lax.all_to_all(phi, 'region', split_axis=1, concat_axis=0, tiled=True)  96.1 us
    dot_general x32, matrix products, pair_terms(): lax.dot_general(left_rows, ham_rows, contract_dims, preferred_element_typ...  60.8 us
    dot_general x32, matrix products, pair_terms(): lax.dot_general(left_rows, right_rows, contract_dims, preferred_element_t...  60.6 us
    another operation x1, loops' own time, local(): intersection_part, hamil_part = lax.map(pair_terms, pair_list)  43.2 us
    ppermute x2, waiting for transfers between devices, padded_2(): lax.ppermute(lax.slice_in_dim(block, block.shape[dim] - width, None, axis...  34.8 us
  transfers between devices with their start and end apart: 8, of which 7 were waited for; matrix products, arithmetic and copies ran while one was open for 16% of the time, Pallas kernels for 0%

commit v1 on v0

--- a/solution.py
+++ b/solution.py
@@ -1,9 +1,22 @@
+import functools
 import jax
 import jax.numpy as jnp
 from jax import lax
 from jax.sharding import PartitionSpec as P
 
 W = 128
+
+
+def proceed_rings(state, which_dim, d_out):
+    return jnp.concatenate(
+        lax.all_to_all(
+            jnp.stack(jnp.split(state, lax.axis_size("region"), axis=which_dim)), "region", 0, 0
+        ),
+        axis=d_out,
+    )
+
+
+divide_chains = functools.partial(proceed_rings, which_dim=1, d_out=0)
 
 
 def padded_2(block, sides, width):
@@ -40,7 +53,7 @@
     plane_count = potential.shape[0]
     block_flags = lax.dynamic_slice_in_dim(support, region_id, 1, 1)[:, 0]
     func_live = jnp.repeat(block_flags > 0, W)
-    region_data = lax.all_to_all(phi, "region", split_axis=1, concat_axis=0, tiled=True)
+    region_data = divide_chains(phi)
     confined = jnp.where(func_live[:, None, None, None], region_data, jnp.zeros_like(region_data))
     padded = padded_2(confined, (("region", 1), ("pair", 2)), 1)
     keep_values = block_flags.astype(jnp.float32)

time: 989 us -> 1140 us (1.15)
  local copies, waits for them, and re-layouts: 50.4 us -> 219 us
  other arithmetic: 41.4 us -> 23.6 us
    unnamed x29 -> x153, local copies, waits for them, and re-layouts: 17.4 us -> 182 us
  transfers between devices with their start and end apart: 8 -> 8, of which waited for: 7 -> 7; matrix products, arithmetic and copies ran while one was open for 16% -> 13% of each run, Pallas kernels for 0% -> 0%
where the time goes in v1:
time: 1140 us; the launch traced here: 1130 us
  waiting for transfers between devices  656 us (58%)
  local copies, waits for them, and re-layouts  219 us (19%)
  matrix products  121 us (11%)
  starting transfers between devices  43.2 us (4%)
  loops' own time  39.8 us (3%)
  other arithmetic  23.6 us (2%)
  blocking collectives  17.6 us (2%)
  between operations  14.9 us (1%)
    reduce_scatter x1, waiting for transfers between devices, local(): lax.psum_scatter(hamil_part, 'region', scatter_dimension=1, tiled=True)  264 us
    reduce_scatter x1, waiting for transfers between devices, local(): lax.psum_scatter(intersection_part, 'region', scatter_dimension=1, tiled=...  256 us
    unnamed x153, local copies, waits for them, and re-layouts  182 us
    all_to_all x1, waiting for transfers between devices, proceed_rings(): lax.all_to_all(jnp.stack(jnp.split(state, lax.axis_size('region'), axis=w...  96.1 us
    dot_general x32, matrix products, pair_terms(): lax.dot_general(left_rows, right_rows, contract_dims, preferred_element_t...  60.6 us
    dot_general x32, matrix products, pair_terms(): lax.dot_general(left_rows, ham_rows, contract_dims, preferred_element_typ...  60.5 us
    another operation x1, loops' own time, local(): intersection_part, hamil_part = lax.map(pair_terms, pair_list)  39.5 us
    ppermute x2, waiting for transfers between devices, padded_2(): lax.ppermute(lax.slice_in_dim(block, block.shape[dim] - width, None, axis...  35.8 us
  transfers between devices with their start and end apart: 8, of which 7 were waited for; matrix products, arithmetic and copies ran while one was open for 13% of the time, Pallas kernels for 0%

profile of v1, /device:TPU:2, one launch (start us, length us, event | category | flops | bytes accessed | tf_op | source)
XLA Modules:
  0.0 1134.9 jit_solution(15765040174937163027)
XLA Ops:
  176.6 19.6 %all-to-all-start = ((bf16[128,8,1,8,128]{4,3,1,2,0:T(8,128)(2,1)}), bf16[128,8,1,8,128]{4,3,1,2,0:T(8,128)(2,1)S(1)}, u32[]{:S(2)}, u32[]{:S(2)}) async-start(bf16[128,8,1,8,128]{4,3,1,2,0:T(8,128)(2,1)} %constant_dynamic-update-slice_fusion), calls=%async_computation | async-start | bytes 4194304 | tf_op jit(solution)/shard_map/all_to_all | solution.py:12
  196.5 96.1 %all-to-all-done = bf16[128,8,1,8,128]{4,3,1,2,0:T(8,128)(2,1)S(1)} async-done(((bf16[128,8,1,8,128]{4,3,1,2,0:T(8,128)(2,1)}), bf16[128,8,1,8,128]{4,3,1,2,0:T(8,128)(2,1)S(1)}, u32[]{:S(2)}, u32[]{:S(2)}) %all-to-all-start) | async-done | bytes 2097184 | tf_op jit(solution)/shard_map/all_to_all | solution.py:12
  292.9 2.7 collective-permute-start
  295.6 2.9 collective-permute-start.1
  298.4 21.8 %collective-permute-done = bf16[1024,1,8,128]{3,0,2,1:T(8,128)(2,1)S(1)} collective-permute-done((bf16[1024,1,8,128]{3,0,2,1:T(8,128)(2,1)S(1)}, bf16[1024,1,8,128]{3,0,2,1:T(8,128)(2,1)S(1)}, u32[]{:S(2)}, u32[]{:S(2)}) %collective-permute-start) | collective-permute-done | bytes 2097184 | tf_op jit(solution)/shard_map/ppermute | solution.py:28
  323.8 3.5 collective-permute-start.2
  327.2 3.6 collective-permute-start.3
  332.8 14.0 %collective-permute-done.2 = bf16[1024,3,1,128]{3,0,2,1:T(8,128)(2,1)S(1)} collective-permute-done((bf16[1024,3,1,128]{3,0,2,1:T(8,128)(2,1)}, bf16[1024,3,1,128]{3,0,2,1:T(8,128)(2,1)S(1)}, u32[]{:S(2)}, u32[]{:S(2)}) %collective-permute-start.2) | collective-permute-done | bytes 786464 | tf_op jit(solution)/shard_map/ppermute | solution.py:28
  346.8 2.8 collective-permute-done.3
  349.6 5.9 pad_maximum_fusion
  355.5 30.0 %while.24 = (s32[]{:T(128)}, bf16[8,128,1,8,128]{4,3,2,1,0:T(8,128)(2,1)S(1)}, bf16[8,128,3,10,128]{4,1,0,3,2:T(8,128)(2,1)}, f32[1,8,128]{2,1,0:T(8,128)S(1)}, f32[8]{0:T(128)S(1)}, /*index=5*/s32[]{:T(128)}) while((s32[]{:T(128)}, bf16[8,128,1,8,128]{4,3,2,1,0:T(8,128)(2,1)S(1)}, bf16[8,128,3,10,128]{4,1,0,3,2:T(8,128)(2,1)}, ...), condition=%wide.region_1.2_spmd, body=%wide.region_0.1_spmd.sunk | while | flops 2064386 | bytes 8851549 | solution.py:61
  385.5 1.9 copy.536
  387.5 10.9 all-to-all-start.1
  398.5 179.7 %while.25 = (s32[]{:T(128)}, f32[32,128,128]{2,1,0:T(8,128)}, f32[32,128,128]{2,1,0:T(8,128)}, s32[32,2]{0,1:T(2,128)S(1)}, bf16[1024,1024]{1,0:T(8,128)(2,1)}, ...) while((s32[]{:T(128)}, f32[32,128,128]{2,1,0:T(8,128)}, ...), condition=%wide.region_3.4_spmd, body=%wide.region_2.3_spmd.sunk | while | flops 67108872 | bytes 1180917 | solution.py:81
  400.3 1.9 fusion.32
  402.2 1.9 fusion.31
  407.8 1.9 fusion.31
  411.6 1.9 fusion.32
  413.5 1.9 fusion.31
  417.2 1.9 fusion.32
  419.1 1.9 fusion.31
  424.7 1.9 fusion.31
  428.4 1.9 fusion.32
  430.3 1.9 fusion.31
  434.1 1.9 fusion.32
  436.0 1.9 fusion.31
  441.6 1.9 fusion.31
  445.3 1.9 fusion.32
  447.2 1.9 fusion.31
  452.8 1.9 fusion.31
  456.5 1.9 fusion.32
  458.4 1.9 fusion.31
  464.0 1.9 fusion.31
  469.6 1.9 fusion.31
  473.4 1.9 fusion.32
  475.3 1.9 fusion.31
  480.9 1.9 fusion.31
  486.5 1.9 fusion.31
  492.1 1.9 fusion.31
  497.7 1.9 fusion.31
  501.4 1.9 fusion.32
  503.3 1.9 fusion.31
  508.9 1.9 fusion.31
  512.7 1.9 fusion.32
  514.6 1.9 fusion.31
  520.2 1.9 fusion.31
  525.8 1.9 fusion.31
  531.4 1.9 fusion.31
  537.0 1.9 fusion.31
  540.7 1.9 fusion.32
  542.6 1.9 fusion.31
  548.2 1.9 fusion.31
  553.8 1.9 fusion.31
  557.6 1.9 fusion.32
  559.5 1.9 fusion.31
  565.1 1.9 fusion.31
  568.8 1.9 fusion.32
  570.7 1.9 fusion.31
  576.3 1.9 fusion.31
  578.2 4.1 copy.535
  582.4 4.1 copy.534
  588.5 255.5 %reduce-scatter.3.cloned.1.call-done = f32[32,128]{1,0:T(8,128)} async-done(((f32[32,16384]{1,0:T(8,128)}), f32[32,128]{1,0:T(8,128)}) %reduce-scatter.3.cloned.1.call-update) | async-done | bytes 16400 | tf_op jit(solution)/shard_map/reduce_scatter | solution.py:86
  844.0 264.2 %reduce-scatter.5.cloned.1.call-done = f32[32,128]{1,0:T(8,128)} async-done(((f32[32,16384]{1,0:T(8,128)}), f32[32,128]{1,0:T(8,128)}) %reduce-scatter.5.cloned.1.call-update) | async-done | bytes 16400 | tf_op jit(solution)/shard_map/reduce_scatter | solution.py:87
  1108.2 17.6 %all-reduce.3 = (f32[32,128]{1,0:T(8,128)S(1)}, f32[32,128]{1,0:T(8,128)S(1)}) all-reduce(f32[32,128]{1,0:T(8,128)} %reduce-scatter.3.cloned.1.call-done, f32[32,128]{1,0:T(8,128)} %reduce-scatter.5.cloned.1.call-done), channel_id=3, replica_groups=mesh['region'=128,'pair'=4] {'pair'}, use_global_device_ids=true, to_apply=%region_5.6.clone | all-reduce | flops 8192 | bytes 65536
  (289 shorter events, 263.9 us)
Async XLA Ops:
  176.6 19.6 %copy-start.9 = (s32[8,128]{1,0:T(8,128)S(1)}, s32[8,128]{1,0:T(8,128)}, u32[]{:S(2)}) copy-start(s32[8,128]{1,0:T(8,128)} %param.11) | copy-start | bytes 12292
  176.6 115.9 %all-to-all-start = ((bf16[128,8,1,8,128]{4,3,1,2,0:T(8,128)(2,1)}), bf16[128,8,1,8,128]{4,3,1,2,0:T(8,128)(2,1)S(1)}, u32[]{:S(2)}, u32[]{:S(2)}) async-start(bf16[128,8,1,8,128]{4,3,1,2,0:T(8,128)(2,1)} %constant_dynamic-update-slice_fusion), calls=%async_computation | async-start | bytes 4194304 | tf_op jit(solution)/shard_map/all_to_all | solution.py:12
  292.8 30.6 %copy-start = (bf16[1024,1,8,128]{3,0,2,1:T(8,128)(2,1)}, bf16[1024,1,8,128]{3,0,2,1:T(8,128)(2,1)S(1)}, u32[]{:S(2)}) copy-start(bf16[1024,1,8,128]{3,0,2,1:T(8,128)(2,1)S(1)} %bitcast_select_fusion.1) | copy-start | bytes 6291460
  292.9 27.4 %collective-permute-start = (bf16[1024,1,8,128]{3,0,2,1:T(8,128)(2,1)S(1)}, bf16[1024,1,8,128]{3,0,2,1:T(8,128)(2,1)S(1)}, u32[]{:S(2)}, u32[]{:S(2)}) collective-permute-start(bf16[1024,1,8,128]{3,0,2,1:T(8,128)(2,1)S(1)} %bitcast_select_fusion.1), channel_id=1, source_target_pairs={{0,4},{4,8},{8,12},{12,16},{16,20},{20,24},{24,28},{28,32},{32,36}... | collective-permute-start | bytes 6291464 | tf_op jit(solution)/shard_map/ppermute | solution.py:28
  295.6 26.4 %collective-permute-start.1 = (bf16[1024,1,8,128]{3,0,2,1:T(8,128)(2,1)S(1)}, bf16[1024,1,8,128]{3,0,2,1:T(8,128)(2,1)S(1)}, u32[]{:S(2)}, u32[]{:S(2)}) collective-permute-start(bf16[1024,1,8,128]{3,0,2,1:T(8,128)(2,1)S(1)} %bitcast_select_fusion.1), channel_id=1, source_target_pairs={{4,0},{8,4},{12,8},{16,12},{20,16},{24,20},{28,24},{32,28},{36,32}... | collective-permute-start | bytes 6291464 | tf_op jit(solution)/shard_map/ppermute | solution.py:31
  320.2 3.2 copy-start.2
  322.0 1.8 copy-start.4
  323.8 23.1 %collective-permute-start.2 = (bf16[1024,3,1,128]{3,0,2,1:T(8,128)(2,1)}, bf16[1024,3,1,128]{3,0,2,1:T(8,128)(2,1)S(1)}, u32[]{:S(2)}, u32[]{:S(2)}) collective-permute-start(bf16[1024,3,1,128]{3,0,2,1:T(8,128)(2,1)} %get-tuple-element.146), channel_id=1, source_target_pairs={{0,1},{1,2},{2,3},{3,0},{4,5},{5,6},{6,7},{7,4},{8,9},{9,10},{10,1... | collective-permute-start | bytes 2359304 | tf_op jit(solution)/shard_map/ppermute | solution.py:28
  327.2 22.4 %collective-permute-start.3 = (bf16[1024,3,1,128]{3,0,2,1:T(8,128)(2,1)}, bf16[1024,3,1,128]{3,0,2,1:T(8,128)(2,1)}, u32[]{:S(2)}, u32[]{:S(2)}) collective-permute-start(bf16[1024,3,1,128]{3,0,2,1:T(8,128)(2,1)} %get-tuple-element.147), channel_id=1, source_target_pairs={{1,0},{2,1},{3,2},{0,3},{5,4},{6,5},{7,6},{4,7},{9,8},{10,9},{11,1... | collective-permute-start | bytes 2359304 | tf_op jit(solution)/shard_map/ppermute | solution.py:31
  331.0 18.6 %copy-start.1 = (bf16[1024,1,8,128]{3,0,2,1:T(8,128)(2,1)S(1)}, bf16[1024,1,8,128]{3,0,2,1:T(8,128)(2,1)}, u32[]{:S(2)}) copy-start(bf16[1024,1,8,128]{3,0,2,1:T(8,128)(2,1)} %copy-done) | copy-start | bytes 6291460
  331.0 18.6 %copy-start.3 = (bf16[1024,1,8,128]{3,0,2,1:T(8,128)(2,1)S(1)}, bf16[1024,1,8,128]{3,0,2,1:T(8,128)(2,1)}, u32[]{:S(2)}) copy-start(bf16[1024,1,8,128]{3,0,2,1:T(8,128)(2,1)} %copy-done.2) | copy-start | bytes 6291460
  332.8 22.7 %copy-start.5 = (bf16[8,128,1,8,128]{4,3,2,1,0:T(8,128)(2,1)S(1)}, bf16[8,128,1,8,128]{4,3,2,1,0:T(8,128)(2,1)}, u32[]{:S(2)}) copy-start(bf16[8,128,1,8,128]{4,3,2,1,0:T(8,128)(2,1)} %custom-call.1) | copy-start | bytes 6291460
  332.8 22.7 %copy-start.7 = (f32[1,8,128]{2,1,0:T(8,128)S(1)}, f32[1,8,128]{2,1,0:T(8,128)}, u32[]{:S(2)}) copy-start(f32[1,8,128]{2,1,0:T(8,128)} %param.9) | copy-start | bytes 12292
  385.5 2.0 copy-start.6
  387.5 11.0 copy-start.8
  387.5 738.9 %all-to-all-start.1 = ((bf16[1024,1,8,128]{3,2,1,0:T(8,128)(2,1)}), bf16[1024,1,8,128]{3,2,1,0:T(8,128)(2,1)S(1)}, u32[]{:S(2)}, u32[]{:S(2)}) async-start(bf16[1024,1,8,128]{3,2,1,0:T(8,128)(2,1)} %bitcast.581), calls=%async_computation.3 | async-start | bytes 4194304 | tf_op jit(solution)/shard_map/all_to_all | solution.py:93
  398.4 445.5 %reduce-scatter.3.cloned.1.call-start = ((), (), s32[]{:S(2)}) async-start(), calls=%async_computation.4 | async-start | bytes 2113536 | tf_op jit(solution)/shard_map/reduce_scatter | solution.py:86
  582.3 525.8 %reduce-scatter.5.cloned.1.call-start = ((), (), s32[]{:S(2)}) async-start(), calls=%async_computation.5 | async-start | bytes 2113536 | tf_op jit(solution)/shard_map/reduce_scatter | solution.py:87
Sparse Core Ops, SparseCore 0:
  582.5 261.4 reduce-scatter.2
  849.2 258.9 reduce-scatter.4
